TPU v7x, 32 devices: a whole 2x2x4 slice. The times are simulated.
32 devices in a mesh: groups: 2 (over y), seq: 8 (over z, x), width: 2 (over core).
Axes of the slice: x: 2, y: 2, z: 4, core: 2. Of those that a mesh axis runs over, the one named last changes fastest.
Arguments:
- span_tokens: bfloat16 [512, 16384], P(('groups', 'seq'), 'width'), parts along dimension 0, may hold values from -6 to 6
- kv_weight: bfloat16 [16384, 1024], P('seq', 'width'), may hold values from -0.046875 to 0.046875
- query_weight: bfloat16 [16384, 8192], P('seq', 'width'), may hold values from -0.046875 to 0.046875
- out_weight: bfloat16 [8192, 16384], P('width', 'seq'), may hold values from -6 to 6
- cache_keys: bfloat16 [16384, 4, 128], P(('groups', 'seq'), 'width'), parts along dimension 0, may hold values from -1000 to 1000
- cache_values: bfloat16 [16384, 4, 128], P(('groups', 'seq'), 'width'), parts along dimension 0, may hold values from -6 to 6
- hidden: bfloat16 [2, 64, 16384], P(None, 'groups', 'seq'), parts along dimension 1, may hold values from -6 to 6
- lengths: int32 [64], P('groups'), parts along dimension 0, may hold values from 1 to 8192
- offset: int32 [2], P('groups'), parts along dimension 0, may hold values from 4096 to 8192
Outputs:
- span_kv: bfloat16 [512, 1024], P(('groups', 'seq'), 'width'), parts along dimension 0
- attended: bfloat16 [2, 64, 16384], P(None, 'groups', ('seq', 'width')), parts along dimension 1
There are 2 independent parts, one for each index of `groups`. A program takes and returns all parts, laid end to end along the dimension named above; an argument that names none is the same for every part. Nothing has to cross between parts.
All inputs are finite; a program needn't handle non-finite values.
Results may differ from a plain program's by a relative error of at most 0.014.
The roundings to bfloat16 on the way count: a program that leaves them out, or rounds other values in their place, can miss the bound.
Values may be sent and summed in bfloat16 or wider, within the bound.
A program may use at most 128 MiB of HBM per device.

v0:
```python
import math

import jax
import jax.numpy as jnp
from jax import lax
from jax.sharding import PartitionSpec as P

HD = 128
QH = 64
KVH = 4
KEY_BLOCK = 256


MASKED_SCORE = -1e30


def combine(earlier, later):
    highest = jnp.maximum(earlier[0], later[0])
    keep_a = jnp.exp(earlier[0] - highest)
    keep_b = jnp.exp(later[0] - highest)
    return (
        highest,
        earlier[1] * keep_a + later[1] * keep_b,
        earlier[2] * keep_a[..., None] + later[2] * keep_b[..., None],
    )


def weigh_block(scores, allowed):
    masked = jnp.where(allowed, scores, MASKED_SCORE)
    highest = jnp.max(masked, axis=-1)
    weights = jnp.where(allowed, jnp.exp(masked - highest[..., None]), 0.0)
    return (highest, jnp.sum(weights, axis=-1), weights.astype(jnp.bfloat16))


def shared_block(queries, key_block, value_block, allowed, factor):
    scores = (
        jnp.einsum("hqd,khd->hqk", queries, key_block, preferred_element_type=jnp.float32) * factor
    )
    highest, weight_sum, weights = weigh_block(scores, allowed)
    summed = jnp.einsum("hqk,khd->hqd", weights, value_block, preferred_element_type=jnp.float32)
    return (highest, weight_sum, summed)


def local(
    span_tokens,
    kv_weight,
    query_weight,
    out_weight,
    cache_keys,
    cache_values,
    hidden,
    lengths,
    offset,
):
    factor = 1.0 / math.sqrt(HD)
    grouped = QH // KVH
    local_heads = kv_weight.shape[1] // (2 * HD)
    query_width = query_weight.shape[1]
    whole_tokens = lax.all_gather(span_tokens, "width", axis=1, tiled=True)
    span_kv = jnp.dot(
        whole_tokens,
        lax.all_gather(kv_weight, "seq", axis=0, tiled=True),
        preferred_element_type=jnp.float32,
    ).astype(jnp.bfloat16)
    step_count = hidden.shape[0]
    branch_count = hidden.shape[1]
    row_count = step_count * branch_count
    flat_rows = row_count * grouped
    states = hidden.reshape(row_count, hidden.shape[2])
    own_rows = lax.psum_scatter(
        jnp.concatenate(
            [
                jnp.dot(states, query_weight, preferred_element_type=jnp.float32),
                jnp.dot(states, kv_weight, preferred_element_type=jnp.float32),
            ],
            axis=1,
        ),
        "seq",
        scatter_dimension=0,
        tiled=True,
    )
    projected = lax.all_gather(own_rows.astype(jnp.bfloat16), "seq", axis=0, tiled=True)
    query_part = projected[:, :query_width]
    queries = query_part.reshape(row_count, local_heads, grouped, HD).transpose(1, 0, 2, 3)
    queries = queries.reshape(local_heads, flat_rows, HD)
    fresh_pairs = projected[:, query_width:].reshape(step_count, branch_count, local_heads, 2, HD)
    visible = jnp.minimum(lengths, offset[0])
    visible_flat = jnp.repeat(jnp.tile(visible, step_count), grouped)
    cache_rows = cache_keys.shape[0]
    blocks = cache_rows // KEY_BLOCK
    anchor = lax.axis_index("seq") * cache_rows
    key_blocks = cache_keys.reshape(blocks, KEY_BLOCK, local_heads, HD)
    value_blocks = cache_values.reshape(blocks, KEY_BLOCK, local_heads, HD)
    leading = anchor + jnp.arange(blocks, dtype=jnp.int32) * KEY_BLOCK

    def cache_step(running, pieces):
        key_block, value_block, begin_at = pieces
        places = begin_at + jnp.arange(KEY_BLOCK, dtype=jnp.int32)
        allowed = (places[None, :] < visible_flat[:, None])[None]
        return (
            combine(running, shared_block(queries, key_block, value_block, allowed, factor)),
            None,
        )

    start_state = (
        jnp.full((local_heads, flat_rows), MASKED_SCORE, jnp.float32),
        jnp.zeros((local_heads, flat_rows), jnp.float32),
        jnp.zeros((local_heads, flat_rows, HD), jnp.float32),
    )
    cache_part, unused = lax.scan(cache_step, start_state, (key_blocks, value_blocks, leading))
    span_pairs = span_kv.reshape(span_kv.shape[0], local_heads, 2, HD)
    everywhere = jnp.ones((1, 1, 1), jnp.bool_)
    span_part = shared_block(queries, span_pairs[:, :, 0], span_pairs[:, :, 1], everywhere, factor)
    local_part = combine(cache_part, span_part)
    grid = query_part.reshape(step_count, branch_count, local_heads, grouped, HD)
    self_scores = (
        jnp.einsum(
            "tbhgd,ubhd->htbgu", grid, fresh_pairs[:, :, :, 0], preferred_element_type=jnp.float32
        )
        * factor
    )
    self_scores = self_scores.reshape(local_heads, flat_rows, step_count)
    causal = jnp.arange(step_count)[None, :] <= jnp.arange(step_count)[:, None]
    allowed = jnp.broadcast_to(
        causal[:, None, None, :], (step_count, branch_count, grouped, step_count)
    )
    allowed = allowed.reshape(flat_rows, step_count)[None]
    highest, weight_sum, weights = weigh_block(self_scores, allowed)
    weights = weights.reshape(local_heads, step_count, branch_count, grouped, step_count)
    summed = jnp.einsum(
        "htbgu,ubhd->htbgd", weights, fresh_pairs[:, :, :, 1], preferred_element_type=jnp.float32
    ).reshape(local_heads, flat_rows, HD)
    own_part = (highest, weight_sum, summed)
    received = (
        lax.all_to_all(local_part[0][None], "seq", split_axis=2, concat_axis=0, tiled=True),
        lax.all_to_all(local_part[1][None], "seq", split_axis=2, concat_axis=0, tiled=True),
        lax.all_to_all(local_part[2][None], "seq", split_axis=2, concat_axis=0, tiled=True),
    )
    highest = jnp.max(received[0], axis=0)
    keep = jnp.exp(received[0] - highest[None])
    folded = (
        highest,
        jnp.sum(received[1] * keep, axis=0),
        jnp.sum(received[2] * keep[..., None], axis=0),
    )
    share = flat_rows // lax.axis_size("seq")
    begin_at = lax.axis_index("seq") * share
    own_slice = tuple((lax.dynamic_slice_in_dim(member, begin_at, share, 1) for member in own_part))
    finished = combine(folded, own_slice)
    ready = (finished[2] / finished[1][..., None]).astype(jnp.bfloat16)
    attended = lax.all_gather(ready, "seq", axis=1, tiled=True)
    flat_out = attended.reshape(local_heads, row_count, grouped, HD).transpose(1, 0, 2, 3)
    flat_out = flat_out.reshape(row_count, query_width)
    partial_out = jnp.dot(flat_out, out_weight, preferred_element_type=jnp.float32)
    partial_out = partial_out.reshape(step_count, branch_count, out_weight.shape[1])
    summed_out = lax.psum_scatter(
        partial_out.astype(jnp.bfloat16), "width", scatter_dimension=2, tiled=True
    )
    return (span_kv, summed_out)


def solution(mesh):
    return jax.shard_map(
        local,
        mesh=mesh,
        in_specs=(
            P(("groups", "seq"), "width"),
            P("seq", "width"),
            P("seq", "width"),
            P("width", "seq"),
            P(("groups", "seq"), "width", None),
            P(("groups", "seq"), "width", None),
            P(None, "groups", "seq"),
            P("groups"),
            P("groups"),
        ),
        out_specs=(P(("groups", "seq"), "width"), P(None, "groups", ("seq", "width"))),
        check_vma=False,
    )
```

profile of v0, /device:TPU:0, one launch (start us, length us, event | category | flops | bytes accessed | tf_op | source)
XLA Modules:
  0.0 394.5 jit_solution(11254233720783330151)
XLA Ops:
  9.0 2.1 fusion.48
  11.0 8.8 %fusion.47 = f32[64,4096]{1,0:T(8,128)S(1)} fusion(bf16[64,2048]{1,0:T(8,128)(2,1)S(1)} %bitcast.126, bf16[2048,4096]{1,0:T(8,128)(2,1)} %param.13), kind=kOutput, calls=%fused_computation.82 | convolution fusion | flops 1073741824 | bytes 18087936 | tf_op jit(solution)/shard_map/dot_general | solution.py:73
  24.1 154.5 %reduce-scatter.3.cloned.1.call-done = f32[8,4608]{1,0:T(8,128)} async-done(((f32[64,4608]{1,0:T(8,128)}), f32[8,4608]{1,0:T(8,128)}) %reduce-scatter.3.cloned.1.call-update) | async-done | bytes 147472 | tf_op jit(solution)/shard_map/reduce_scatter | solution.py:70
  179.4 41.7 %all_gather.14 = bf16[64,4608]{1,0:T(8,128)(2,1)S(1)} all-gather(bf16[8,4608]{1,0:T(8,128)(2,1)S(1)} %convert_element_type.23), channel_id=1, replica_groups=mesh['groups'=2,'seq'=8,'width'=2] {'seq'}, dimensions={0}, use_global_device_ids=true | all-gather | bytes 663552 | tf_op jit(solution)/shard_map/all_gather | solution.py:82
  222.0 37.8 %while.15 = (s32[]{:T(128)}, f32[2,1024]{1,0:T(2,128)}, f32[2,1024]{1,0:T(2,128)}, f32[2,1024,128]{2,1,0:T(8,128)}, s32[4]{0:T(128)}, /*index=5*/bf16[4,256,2,12...) while((s32[]{:T(128)}, f32[2,1024]{1,0:T(2,128)}, ...), condition=%wide.region_4.5_spmd.clone, body=%wide.region_1.4_spmd.clone.sunk | while | flops 276574464 | bytes 10881428 | solution.py:110
  222.8 1.3 dynamic_slice.40
  227.9 2.2 fusion.69
  231.0 1.3 dynamic_slice.40
  235.5 1.3 fusion.68
  236.8 3.2 fusion.69
  240.9 1.3 dynamic_slice.40
  245.3 1.3 fusion.68
  246.7 3.2 fusion.69
  250.8 1.3 dynamic_slice.40
  255.2 1.3 fusion.68
  256.6 3.2 fusion.69
  259.8 18.0 %all-gather.5.cloned.1.call-done = bf16[16384,512]{1,0:T(8,128)(2,1)} async-done(((bf16[2048,512]{1,0:T(8,128)(2,1)}), bf16[16384,512]{1,0:T(8,128)(2,1)}) %all-gather.5.cloned.1.call-update) | async-done | bytes 16777232 | tf_op jit(solution)/shard_map/all_gather | solution.py:62
  277.8 9.0 %convolution_convert_fusion = bf16[32,512]{1,0:T(8,128)(2,1)S(1)} fusion(bf16[32,16384]{1,0:T(8,128)(2,1)} %all-gather.3.cloned.1.call-done, bf16[16384,512]{1,0:T(8,128)(2,1)} %all-gather.5.cloned.1.call-done), kind=kOutput, calls=%fused_computation.42 | convolution fusion | flops 536887296 | bytes 17858560 | tf_op jit(solution)/shard_map/dot_general | solution.py:60
  288.2 1.9 reduce.3
  291.0 3.3 all-to-all-start.2
  294.7 1.9 reduce.5
  297.5 3.3 all-to-all-done.2
  300.8 3.5 all-to-all-start.1
  305.2 1.8 copy.108
  307.0 3.5 all-to-all-done.1
  310.6 3.6 all-to-all-start
  314.3 1.4 fusion.45
  320.4 16.8 %all-to-all-done = f32[1,2,1024,128]{3,1,0,2:T(2,128)S(1)} async-done(((f32[1,2,1024,128]{3,1,0,2:T(2,128)}), f32[1,2,1024,128]{3,1,0,2:T(2,128)S(1)}, u32[]{:S(2)}, u32[]{:S(2)}) %all-to-all-start) | async-done | bytes 1048608 | tf_op jit(solution)/shard_map/all_to_all | solution.py:137
  337.2 1.4 multiply_reduce_fusion
  339.1 31.5 %all_gather.15 = bf16[2,1024,128]{2,0,1:T(2,128)(2,1)S(1)} all-gather(bf16[2,128,128]{2,0,1:T(2,128)(2,1)S(1)} %fusion.34), channel_id=1, replica_groups=mesh['groups'=2,'seq'=8,'width'=2] {'seq'}, dimensions={1}, use_global_device_ids=true | all-gather | bytes 589824 | tf_op jit(solution)/shard_map/all_gather | solution.py:151
  371.0 9.5 %fusion.20 = bf16[2,32,2048]{2,1,0:T(8,128)(2,1)} fusion(bf16[2,32,4096]{2,1,0:T(8,128)(2,1)S(1)} %dot_general.39, bf16[4096,2048]{1,0:T(8,128)(2,1)} %param.14), kind=kOutput, calls=%fused_computation.32 | convolution fusion | flops 1073872896 | bytes 17563648 | tf_op jit(solution)/shard_map/dot_general | solution.py:154
  380.6 6.3 %reduce-scatter.5.cloned.1.call-done = bf16[2,32,1024]{2,1,0:T(8,128)(2,1)} async-done(((bf16[2,32,2048]{2,1,0:T(8,128)(2,1)}), bf16[2,32,1024]{2,1,0:T(8,128)(2,1)}) %reduce-scatter.5.cloned.1.call-update) | async-done | bytes 131088 | tf_op jit(solution)/shard_map/reduce_scatter | solution.py:156
  (106 shorter events, 32.8 us)
Async XLA Ops:
  8.0 1.0 copy-start
  8.0 170.5 %reduce-scatter.3.cloned.1.call-start = ((), (), s32[]{:S(2)}) async-start(), calls=%async_computation.7 | async-start | bytes 1327104 | tf_op jit(solution)/shard_map/reduce_scatter | solution.py:70
  20.9 1.9 copy-start.7
  20.9 238.9 %all-gather.3.cloned.1.call-start = ((), (), s32[]{:S(2)}) async-start(), calls=%async_computation.5 | async-start | bytes 1572864 | tf_op jit(solution)/shard_map/all_gather | solution.py:59
  21.5 256.3 %all-gather.5.cloned.1.call-start = ((), (), s32[]{:S(2)}) async-start(), calls=%async_computation.6 | async-start | bytes 18874368 | tf_op jit(solution)/shard_map/all_gather | solution.py:62
  221.1 0.8 copy-start.2
  259.8 27.5 %copy-start.4 = (f32[2,1024]{1,0:T(2,128)S(1)}, f32[2,1024]{1,0:T(2,128)}, u32[]{:S(2)}) copy-start(f32[2,1024]{1,0:T(2,128)} %get-tuple-element.52) | copy-start | bytes 24580
  259.8 27.5 %copy-start.5 = (f32[2,1024]{1,0:T(2,128)S(1)}, f32[2,1024]{1,0:T(2,128)}, u32[]{:S(2)}) copy-start(f32[2,1024]{1,0:T(2,128)} %get-tuple-element.53) | copy-start | bytes 24580
  286.8 9.7 %copy-start.6 = (bf16[32,512]{1,0:T(8,128)(2,1)}, bf16[32,512]{1,0:T(8,128)(2,1)S(1)}, u32[]{:S(2)}) copy-start(bf16[32,512]{1,0:T(8,128)(2,1)S(1)} %convolution_convert_fusion) | copy-start | bytes 98308
  287.3 16.9 %copy-start.3 = (f32[2,1024,128]{2,1,0:T(8,128)S(1)}, f32[2,1024,128]{2,1,0:T(8,128)}, u32[]{:S(2)}) copy-start(f32[2,1024,128]{2,1,0:T(8,128)} %get-tuple-element.51) | copy-start | bytes 3145732
  291.0 9.8 %all-to-all-start.2 = ((f32[8,1,256]{2,1,0:T(1,128)}), f32[8,1,256]{2,1,0:T(1,128)S(1)}, u32[]{:S(2)}, u32[]{:S(2)}) async-start(f32[8,1,256]{2,1,0:T(1,128)} %reshape.135), calls=%async_computation.3 | async-start | bytes 16384 | tf_op jit(solution)/shard_map/all_to_all | solution.py:136
  300.8 9.8 %all-to-all-start.1 = ((f32[8,1,256]{2,1,0:T(1,128)}), f32[8,1,256]{2,1,0:T(1,128)S(1)}, u32[]{:S(2)}, u32[]{:S(2)}) async-start(f32[8,1,256]{2,1,0:T(1,128)} %reshape.133), calls=%async_computation.2 | async-start | bytes 16384 | tf_op jit(solution)/shard_map/all_to_all | solution.py:135
  305.2 9.0 %slice-start = ((bf16[64,4608]{1,0:T(8,128)(2,1)}), bf16[64,512]{1,0:T(8,128)(2,1)S(1)}, s32[]{:S(2)}) async-start(bf16[64,4608]{1,0:T(8,128)(2,1)} %copy-done.2), calls=%async_computation.9 | async-start | bytes 131072 | tf_op jit(solution)/shard_map/slice | solution.py:86
  310.6 26.7 %all-to-all-start = ((f32[1,2,1024,128]{3,1,0,2:T(2,128)}), f32[1,2,1024,128]{3,1,0,2:T(2,128)S(1)}, u32[]{:S(2)}, u32[]{:S(2)}) async-start(f32[1,2,1024,128]{3,1,0,2:T(2,128)} %copy.108), calls=%async_computation.1 | async-start | bytes 2097152 | tf_op jit(solution)/shard_map/all_to_all | solution.py:137
  314.1 72.7 %reduce-scatter.5.cloned.1.call-start = ((), (), s32[]{:S(2)}) async-start(), calls=%async_computation.8 | async-start | bytes 393216 | tf_op jit(solution)/shard_map/reduce_scatter | solution.py:156
  371.0 15.9 %copy-start.1 = (bf16[2,32,2048]{2,1,0:T(8,128)(2,1)S(1)}, bf16[2,32,2048]{2,1,0:T(8,128)(2,1)}, u32[]{:S(2)}) copy-start(bf16[2,32,2048]{2,1,0:T(8,128)(2,1)} %param.17) | copy-start | bytes 786436
Sparse Core Ops, SparseCore 0:
  21.1 157.4 reduce-scatter.2
Sparse Core Ops, SparseCore 1:
  23.0 11.6 all-gather.2
  36.6 241.1 all-gather.4
  380.7 6.2 reduce-scatter.4
where the time goes:
time: 395 us; the launch traced here: 394 us
  waiting for transfers between devices  203 us (51%)
  blocking collectives  73.2 us (19%)
  matrix products  46.8 us (12%)
  local copies, waits for them, and re-layouts  23.3 us (6%)
  other arithmetic  20.3 us (5%)
  between operations  16.7 us (4%)
  starting transfers between devices  10.6 us (3%)
    reduce_scatter x1, waiting for transfers between devices, local(): lax.psum_scatter(jnp.concatenate([jnp.dot(states, query_weight, preferred...  154 us
    all_gather x1, blocking collectives, local(): lax.all_gather(own_rows.astype(jnp.bfloat16), 'seq', axis=0, tiled=True)  41.7 us
    all_gather x1, blocking collectives, local(): attended = lax.all_gather(ready, 'seq', axis=1, tiled=True)  31.5 us
    all_gather x1, waiting for transfers between devices, local(): lax.all_gather(kv_weight, 'seq', axis=0, tiled=True)  18 us
    all_to_all x1, waiting for transfers between devices, local(): lax.all_to_all(local_part[2][None], 'seq', split_axis=2, concat_axis=0, t...  16.8 us
    dot_general x5, matrix products, shared_block(): jnp.einsum('hqk,khd->hqd', weights, value_block, preferred_element_type=j...  12.8 us
    dynamic_slice x8, local copies, waits for them, and re-layouts, local(): lax.scan(cache_step, start_state, (key_blocks, value_blocks, leading))  9.75 us
    dot_general x1, matrix products, local(): jnp.dot(flat_out, out_weight, preferred_element_type=jnp.float32)  9.53 us
  transfers between devices with their start and end apart: 7, of which 6 were waited for; matrix products, arithmetic and copies ran while one was open for 13% of the time, Pallas kernels for 0%

commit v1 on v0

v1 whole, which is shorter than its diff:
```python
import functools
import math

import jax
import jax.numpy as jnp
from jax import lax
from jax.experimental import pallas as pl
from jax.experimental.pallas import tpu as pltpu
from jax.sharding import PartitionSpec as P

HD = 128
QH = 64
KVH = 4
MASKED = -1e30
MESH = pl.DeviceIdType.MESH
NT = (((1,), (1,)), ((), ()))


def remote(src, dst, send, recv, device):
    return pltpu.make_async_remote_copy(
        src_ref=src, dst_ref=dst, send_sem=send, recv_sem=recv, device_id=device, device_id_type=MESH
    )


def layer(
    n, steps, tile,
    tok_ref, hid_ref, vis_ref, kvw_ref, qw_ref, ow_ref, ck_ref, cv_ref,
    span_ref, out_ref,
    qw_v, kvw_v, ow_v, ck_v, cv_v, vt_v, vts_v,
    part, qrecv, tokg, spart, srecv, gath, obuf, orecv, mlbuf, mlrecv, att, xbuf, xrecv,
    qw_sem, kvw_sem, ow_sem, c_sem, own_sem,
    tok_s, tok_r, fwd_s, q_s, q_r, sp_s, sp_r, g_s, g_r, o_s, o_r, ml_s, ml_r, a_s, a_r, x_s, x_r,
):
    f32, bf16 = jnp.float32, jnp.bfloat16
    me = lax.axis_index("seq")
    w = lax.axis_index("width")
    other = 1 - w
    r = part.shape[1]
    heads = kvw_v.shape[1] // (2 * HD)
    grouped = QH // KVH
    qcols = qw_ref.shape[1]
    ccols = part.shape[2]
    tiles = qcols // tile
    feats = hid_ref.shape[1]
    lanes = grouped * r
    factor = 1.0 / math.sqrt(HD)
    per_half = tok_ref.shape[1] // feats
    toks = tok_ref.shape[0]

    def peers(body):
        def step(d, carry):
            body(lax.rem(me + d, n))
            return carry

        lax.fori_loop(1, n, step, 0)

    def qw_copy(t):
        cols = pl.ds(pl.multiple_of(t * tile, tile), tile)
        return pltpu.make_async_copy(qw_ref.at[:, cols], qw_v.at[t], qw_sem.at[t])

    for t in range(tiles):
        qw_copy(t).start()
    kvw_copy = pltpu.make_async_copy(kvw_ref, kvw_v, kvw_sem)
    kvw_copy.start()
    ck_copy = pltpu.make_async_copy(ck_ref, ck_v, c_sem.at[0])
    cv_copy = pltpu.make_async_copy(cv_ref, cv_v, c_sem.at[1])
    ck_copy.start()
    cv_copy.start()
    ow_parts = ow_sem.shape[0]
    ow_rows = ow_ref.shape[0] // ow_parts
    ow_copies = [
        pltpu.make_async_copy(
            ow_ref.at[pl.ds(k * ow_rows, ow_rows)], ow_v.at[pl.ds(k * ow_rows, ow_rows)], ow_sem.at[k]
        )
        for k in range(ow_parts)
    ]
    for copy in ow_copies:
        copy.start()

    barrier = pltpu.get_barrier_semaphore()
    peers(
        lambda j: pl.semaphore_signal(barrier, inc=1, device_id={"seq": j}, device_id_type=MESH)
    )
    pl.semaphore_signal(barrier, inc=1, device_id={"width": other}, device_id_type=MESH)
    pl.semaphore_wait(barrier, n)

    def tok_copy(k):
        dest = w * per_half + k
        cols = pl.ds(pl.multiple_of(k * feats, 128), feats)
        return dest, cols

    def tok_send(k, carry):
        dest, cols = tok_copy(k)

        @pl.when(dest != me)
        def _():
            remote(
                tok_ref.at[:, cols], tokg.at[me], tok_s.at[k], tok_r.at[me], {"seq": dest}
            ).start()

        @pl.when(dest == me)
        def _():
            pltpu.make_async_copy(tok_ref.at[:, cols], tokg.at[me], own_sem).start()

        return carry

    lax.fori_loop(0, per_half, tok_send, 0)

    def q_send(value, cols):
        for j in range(n):
            part[j, :, cols] = value[j * r : (j + 1) * r]
        peers(
            lambda j: remote(
                part.at[j, :, cols], qrecv.at[me, :, cols], q_s.at[j], q_r.at[me], {"seq": j}
            ).start()
        )

    def q_tile(t, carry):
        qw_copy(t).wait()
        value = jnp.dot(hid_ref[...], qw_v[t], preferred_element_type=f32)
        q_send(value, pl.ds(pl.multiple_of(t * tile, tile), tile))
        return carry

    lax.fori_loop(0, tiles, q_tile, 0)
    kvw_copy.wait()
    q_send(
        jnp.dot(hid_ref[...], kvw_v[...], preferred_element_type=f32), pl.ds(qcols, ccols - qcols)
    )

    holder = w == me // per_half

    def tok_recv(i, device):
        return remote(tokg.at[i], tokg.at[i], fwd_s.at[i], tok_r.at[i], device)

    @pl.when(holder)
    def _():
        pltpu.make_async_copy(tokg.at[me], tokg.at[me], own_sem).wait()

        def pass_on(d, carry):
            i = lax.rem(me + d, n)

            @pl.when(i != me)
            def _():
                tok_recv(i, {"seq": i}).wait_recv()

            tok_recv(i, {"width": other}).start()
            return carry

        lax.fori_loop(0, n, pass_on, 0)

    @pl.when(jnp.logical_not(holder))
    def _():
        def take(i, carry):
            tok_recv(i, {"width": other}).wait_recv()
            return carry

        lax.fori_loop(0, n, take, 0)

    group = min(n, 8)

    def span_chunk(c, carry):
        rows = tokg[pl.ds(c * group, group)].reshape(group * toks, feats)
        value = jnp.dot(rows, kvw_v[...], preferred_element_type=f32)
        spart[pl.ds(c * group, group)] = value.reshape(group, toks, value.shape[1])
        return carry

    lax.fori_loop(0, n // group, span_chunk, 0)
    peers(
        lambda j: remote(spart.at[j], srecv.at[me], sp_s.at[j], sp_r.at[me], {"seq": j}).start()
    )

    qrecv[me] = part[me]
    peers(lambda j: remote(part.at[j], qrecv.at[j], q_s.at[j], q_r.at[j], {"seq": j}).wait_recv())
    total = lax.fori_loop(1, n, lambda i, acc: acc + qrecv[i], qrecv[0])
    gath[me] = jnp.concatenate(
        [total[:, c * HD : (c + 1) * HD] for c in range(ccols // HD)], axis=0
    ).astype(bf16)
    peers(lambda j: remote(gath.at[me], gath.at[me], g_s.at[j], g_r.at[me], {"seq": j}).start())

    ck_copy.wait()
    cv_copy.wait()
    for h in range(heads):
        vt_v[h] = cv_v[:, h * HD : (h + 1) * HD].astype(f32).T.astype(bf16)

    srecv[me] = spart[me]
    peers(lambda j: remote(spart.at[j], srecv.at[j], sp_s.at[j], sp_r.at[j], {"seq": j}).wait_recv())
    span = lax.fori_loop(1, n, lambda i, acc: acc + srecv[i], srecv[0]).astype(bf16)
    span_ref[...] = span
    for h in range(heads):
        vts_v[h] = span[:, (2 * h + 1) * HD : (2 * h + 2) * HD].astype(f32).T.astype(bf16)

    peers(lambda j: remote(gath.at[j], gath.at[j], g_s.at[j], g_r.at[j], {"seq": j}).wait_recv())

    slots = ck_v.shape[0]
    anchor = me * slots
    jc = max(1, min(n, 256 // lanes))
    width = jc * lanes

    def attend(c, carry):
        visible = vis_ref[pl.ds(c, 1)] - anchor
        for h in range(heads):
            q = gath[pl.ds(c * jc, jc), h * lanes : (h + 1) * lanes, :].reshape(width, HD)
            s1 = lax.dot_general(
                ck_v[:, h * HD : (h + 1) * HD], q, NT, preferred_element_type=f32
            ) * factor
            s2 = lax.dot_general(
                span_ref[:, 2 * h * HD : (2 * h + 1) * HD], q, NT, preferred_element_type=f32
            ) * factor
            place = lax.broadcasted_iota(jnp.int32, s1.shape, 0)
            s1 = jnp.where(place < visible, s1, MASKED)
            m = jnp.maximum(
                jnp.max(s1, axis=0, keepdims=True), jnp.max(s2, axis=0, keepdims=True)
            )
            w1 = jnp.exp(s1 - m)
            w2 = jnp.exp(s2 - m)
            l = jnp.sum(w1, axis=0, keepdims=True) + jnp.sum(w2, axis=0, keepdims=True)
            o = jnp.dot(vt_v[h], w1.astype(bf16), preferred_element_type=f32)
            o = (o + jnp.dot(vts_v[h], w2.astype(bf16), preferred_element_type=f32)).astype(bf16)
            for k in range(jc):
                cut = slice(k * lanes, (k + 1) * lanes)
                obuf[c * jc + k, h] = o[:, cut]
                mlbuf[c * jc + k, h : h + 1] = m[:, cut]
                mlbuf[c * jc + k, heads + h : heads + h + 1] = l[:, cut]
        for k in range(jc):
            j = c * jc + k

            @pl.when(j != me)
            def _():
                remote(mlbuf.at[j], mlrecv.at[me], ml_s.at[j], ml_r.at[me], {"seq": j}).start()
                remote(obuf.at[j], orecv.at[me], o_s.at[j], o_r.at[me], {"seq": j}).start()

        return carry

    lax.fori_loop(0, n // jc, attend, 0)

    per_step = n // steps
    step = me // per_step
    fresh = []
    for h in range(heads):
        q = gath[me, h * lanes : (h + 1) * lanes, :]
        base = (heads * grouped + 2 * h) * r
        pairs = [
            gath[u * per_step + lax.rem(me, per_step)].astype(f32) for u in range(steps)
        ]
        keys = jnp.concatenate([p[base : base + r] for p in pairs], axis=0)
        values = jnp.concatenate([p[base + r : base + 2 * r] for p in pairs], axis=0)
        s = lax.dot_general(keys.astype(bf16), q, NT, preferred_element_type=f32) * factor
        row = lax.broadcasted_iota(jnp.int32, s.shape, 0)
        lane = lax.broadcasted_iota(jnp.int32, s.shape, 1)
        allowed = jnp.logical_and(lax.rem(row, r) == lax.rem(lane, r), row // r <= step)
        s = jnp.where(allowed, s, MASKED)
        m = jnp.max(s, axis=0, keepdims=True)
        e = jnp.where(allowed, jnp.exp(s - m), 0.0)
        l = jnp.sum(e, axis=0, keepdims=True)
        o = jnp.dot(values.T.astype(bf16), e.astype(bf16), preferred_element_type=f32)
        fresh.append((m, l, o))

    orecv[me] = obuf[me]
    mlrecv[me] = mlbuf[me]

    def o_wait(j):
        remote(mlbuf.at[j], mlrecv.at[j], ml_s.at[j], ml_r.at[j], {"seq": j}).wait_recv()
        remote(obuf.at[j], orecv.at[j], o_s.at[j], o_r.at[j], {"seq": j}).wait_recv()

    peers(o_wait)
    pieces = []
    for h in range(heads):
        m0, l0, o0 = fresh[h]
        top = lax.fori_loop(0, n, lambda i, a: jnp.maximum(a, mlrecv[i, h : h + 1]), m0)
        keep = jnp.exp(m0 - top)

        def fold(i, acc):
            k = jnp.exp(mlrecv[i, h : h + 1] - top)
            return acc[0] + mlrecv[i, heads + h : heads + h + 1] * k, acc[1] + orecv[i, h].astype(f32) * k

        l, o = lax.fori_loop(0, n, fold, (l0 * keep, o0 * keep))
        ready = (o / l).T
        pieces += [ready[g * r : (g + 1) * r] for g in range(grouped)]
    att[me] = jnp.concatenate(pieces, axis=1).astype(bf16)
    peers(lambda j: remote(att.at[me], att.at[me], a_s.at[j], a_r.at[me], {"seq": j}).start())
    for copy in ow_copies:
        copy.wait()
    peers(lambda j: remote(att.at[j], att.at[j], a_s.at[j], a_r.at[j], {"seq": j}).wait_recv())
    rows = jnp.concatenate([att[j].astype(f32) for j in range(n)], axis=0).astype(bf16)
    own = out_ref.shape[1]
    cut = min(own, 256)

    def out_tile(side, c):
        cols = pl.ds(pl.multiple_of(side * own + c * cut, 128), cut)
        return jnp.dot(rows, ow_v[:, cols], preferred_element_type=f32)

    for c in range(own // cut):
        xbuf[:, c * cut : (c + 1) * cut] = out_tile(other, c).astype(bf16)
    swap = remote(xbuf, xrecv, x_s, x_r, {"width": other})
    swap.start()
    kept = [out_tile(w, c) for c in range(own // cut)]
    swap.wait_recv()
    for c in range(own // cut):
        there = slice(c * cut, (c + 1) * cut)
        out_ref[:, there] = (kept[c] + xrecv[:, there].astype(f32)).astype(bf16)

    def tok_sent(k, carry):
        dest, cols = tok_copy(k)

        @pl.when(dest != me)
        def _():
            remote(
                tok_ref.at[:, cols], tokg.at[me], tok_s.at[k], tok_r.at[me], {"seq": dest}
            ).wait_send()

        return carry

    lax.fori_loop(0, per_half, tok_sent, 0)

    @pl.when(holder)
    def _():
        def passed(i, carry):
            tok_recv(i, {"width": other}).wait_send()
            return carry

        lax.fori_loop(0, n, passed, 0)

    def sent(j):
        at = {"seq": j}
        remote(part.at[j], qrecv.at[me], q_s.at[j], q_r.at[me], at).wait_send()
        remote(spart.at[j], srecv.at[me], sp_s.at[j], sp_r.at[me], at).wait_send()
        remote(gath.at[me], gath.at[me], g_s.at[j], g_r.at[me], at).wait_send()
        remote(mlbuf.at[j], mlrecv.at[me], ml_s.at[j], ml_r.at[me], at).wait_send()
        remote(obuf.at[j], orecv.at[me], o_s.at[j], o_r.at[me], at).wait_send()
        remote(att.at[me], att.at[me], a_s.at[j], a_r.at[me], at).wait_send()

    peers(sent)
    swap.wait_send()


def local(
    mesh,
    span_tokens, kv_weight, query_weight, out_weight, cache_keys, cache_values, hidden, lengths, offset,
):
    n = mesh.shape["seq"]
    steps, branches, feats = hidden.shape
    rows = steps * branches
    r = rows // n
    grouped = QH // KVH
    lanes = grouped * r
    toks = span_tokens.shape[0]
    kvc = kv_weight.shape[1]
    heads = kvc // (2 * HD)
    qcols = query_weight.shape[1]
    ccols = qcols + kvc
    tile = min(qcols, 512)
    slots = cache_keys.shape[0]
    own = out_weight.shape[1] // mesh.shape["width"]
    f32, bf16 = jnp.float32, jnp.bfloat16

    jc = max(1, min(n, 256 // lanes))
    visible = jnp.tile(jnp.minimum(lengths, offset[0]), steps).reshape(n, 1, r)
    visible = jnp.broadcast_to(visible, (n, grouped, r)).reshape(n // jc, jc * lanes)

    vm = pl.BlockSpec(memory_space=pltpu.VMEM)
    hbm = pl.BlockSpec(memory_space=pl.ANY)
    dma = pltpu.SemaphoreType.DMA
    ow_parts = 8
    span_kv, out = pl.pallas_call(
        functools.partial(layer, n, steps, tile),
        out_shape=(
            jax.ShapeDtypeStruct((toks, kvc), bf16),
            jax.ShapeDtypeStruct((rows, own), bf16),
        ),
        in_specs=[vm, vm, vm, hbm, hbm, hbm, hbm, hbm],
        out_specs=(vm, vm),
        scratch_shapes=[
            pltpu.VMEM((qcols // tile, feats, tile), bf16),
            pltpu.VMEM((feats, kvc), bf16),
            pltpu.VMEM(out_weight.shape, bf16),
            pltpu.VMEM((slots, heads * HD), bf16),
            pltpu.VMEM((slots, heads * HD), bf16),
            pltpu.VMEM((heads, HD, slots), bf16),
            pltpu.VMEM((heads, HD, toks), bf16),
            pltpu.VMEM((n, r, ccols), f32),
            pltpu.VMEM((n, r, ccols), f32),
            pltpu.VMEM((n, toks, feats), bf16),
            pltpu.VMEM((n, toks, kvc), f32),
            pltpu.VMEM((n, toks, kvc), f32),
            pltpu.VMEM((n, ccols // HD * r, HD), bf16),
            pltpu.VMEM((n, heads, HD, lanes), bf16),
            pltpu.VMEM((n, heads, HD, lanes), bf16),
            pltpu.VMEM((n, 2 * heads, lanes), f32),
            pltpu.VMEM((n, 2 * heads, lanes), f32),
            pltpu.VMEM((n, r, qcols), bf16),
            pltpu.VMEM((rows, own), bf16),
            pltpu.VMEM((rows, own), bf16),
            dma((qcols // tile,)), dma, dma((ow_parts,)), dma((2,)), dma,
            dma((n,)), dma((n,)), dma((n,)), dma((n,)), dma((n,)), dma((n,)), dma((n,)),
            dma((n,)), dma((n,)), dma((n,)), dma((n,)), dma((n,)), dma((n,)), dma((n,)), dma((n,)),
            dma, dma,
        ],
        compiler_params=pltpu.CompilerParams(
            collective_id=0, has_side_effects=True, vmem_limit_bytes=62 * 1024 * 1024
        ),
    )(
        span_tokens,
        hidden.reshape(rows, feats),
        visible,
        kv_weight,
        query_weight,
        out_weight,
        cache_keys.reshape(slots, heads * HD),
        cache_values.reshape(slots, heads * HD),
    )
    return span_kv, out.reshape(steps, branches, own)


def solution(mesh):
    return jax.shard_map(
        functools.partial(local, mesh),
        mesh=mesh,
        in_specs=(
            P(("groups", "seq"), "width"),
            P("seq", "width"),
            P("seq", "width"),
            P("width", "seq"),
            P(("groups", "seq"), "width", None),
            P(("groups", "seq"), "width", None),
            P(None, "groups", "seq"),
            P("groups"),
            P("groups"),
        ),
        out_specs=(P(("groups", "seq"), "width"), P(None, "groups", ("seq", "width"))),
        check_vma=False,
    )
```

time: 395 us -> 113 us (0.29)
  waiting for transfers between devices: 203 us -> 0 us
  Pallas kernels: 0 us -> 104 us
  blocking collectives: 73.2 us -> 0 us
  matrix products: 46.8 us -> 0 us
  other arithmetic: 20.3 us -> 0.66 us
  local copies, waits for them, and re-layouts: 23.3 us -> 6.07 us
  between operations: 16.7 us -> 1.29 us
  starting transfers between devices: 10.6 us -> 0 us
    reduce_scatter x2 -> x0, waiting for transfers between devices: 161 us -> none  [the longest x1 154 us: local(): lax.psum_scatter(jnp.concatenate([jnp.dot(states, query_weight, preferred...]
    pallas_call x0 -> x1, Pallas kernels: none -> 104 us  [local(): pl.pallas_call(functools.partial(layer, n, steps, tile), out_shape=(jax.S...]
    all_gather x2 -> x0, blocking collectives: 73.2 us -> none  [the longest x1 41.7 us: local(): lax.all_gather(own_rows.astype(jnp.bfloat16), 'seq', axis=0, tiled=True)]
    dot_general x16 -> x0, matrix products: 46.8 us -> none  [the longest x5 12.8 us: shared_block(): jnp.einsum('hqk,khd->hqd', weights, value_block, preferred_element_type=j...]
    all_to_all x3 -> x0, waiting for transfers between devices: 23.6 us -> none  [the longest x1 16.8 us: local(): lax.all_to_all(local_part[2][None], 'seq', split_axis=2, concat_axis=0, t...]
    all_gather x2 -> x0, waiting for transfers between devices: 18 us -> none  [the longest x1 18 us: local(): lax.all_gather(kv_weight, 'seq', axis=0, tiled=True)]
    all_to_all x3 -> x0, starting transfers between devices: 10.4 us -> none  [the longest x1 3.56 us: local(): lax.all_to_all(local_part[2][None], 'seq', split_axis=2, concat_axis=0, t...]
    dynamic_slice x9 -> x0, local copies, waits for them, and re-layouts: 9.77 us -> none  [the longest x8 9.75 us: local(): lax.scan(cache_step, start_state, (key_blocks, value_blocks, leading))]
  transfers between devices with their start and end apart: 7 -> 0, of which waited for: 6 -> 0; matrix products, arithmetic and copies ran while one was open for 13% -> 0% of each run, Pallas kernels for 0% -> 0%
where the time goes in v1:
time: 113 us; the launch traced here: 112 us
  Pallas kernels  104 us (92%)
  local copies, waits for them, and re-layouts  6.07 us (5%)
  between operations  1.29 us (1%)
    pallas_call x1, Pallas kernels, local(): pl.pallas_call(functools.partial(layer, n, steps, tile), out_shape=(jax.S...  104 us
    unnamed x2, local copies, waits for them, and re-layouts  2.94 us
    reshape x1, local copies, waits for them, and re-layouts, local(): cache_values.reshape(slots, heads * HD)  2.33 us

profile of v1, /device:TPU:0, one launch (start us, length us, event | category | flops | bytes accessed | tf_op | source)
XLA Modules:
  0.0 112.2 jit_solution(3789992184238266551)
XLA Ops:
  1.3 0.7 broadcast_minimum_fusion
  1.9 0.1 tile.10
  2.0 0.7 reshape.28.vis_ref
  2.7 2.3 %copy_bitcast_fusion = (bf16[1024,256]{1,0:T(8,128)(2,1)}, bf16[1024,256]{1,0:T(8,128)(2,1)}) fusion(bf16[128,8,2,128]{3,2,1,0:T(2,128)(2,1)} %bitcast.11, bf16[128,8,2,128]{3,2,1,0:T(2,128)(2,1)} %bitcast.12), kind=kLoop, calls=%fused_computation | loop fusion | bytes 2097152 | tf_op jit(solution)/shard_map/reshape | solution.py:409
  5.1 104.2 %shard_map.104 = (bf16[32,512]{1,0:T(8,128)(2,1)}, bf16[64,1024]{1,0:T(8,128)(2,1)}) custom-call(bf16[32,8192]{1,0:T(8,128)(2,1)} %tok_ref.1, bf16[64,2048]{1,0:T(8,128)(2,1)} %bitcast.13, s32[4,256]{1,0:T(4,128)} %reshape.28.vis_ref, bf16[2048,512]{1,0:T(8,128)(2,1)} %kvw_ref.1, bf16[2048,4096]{1,0:T(8,128)(2,1)} %qw_ref.1, bf16[4096,2048]{1,0:T(8,128)(2,1)} %ow_ref.1, ...), custom_call_target="tpu_custom_call" | custom-call | tf_op jit(solution)/shard_map/pallas_call | solution.py:364
  109.3 1.4 %copy.18 = bf16[32,512]{1,0:T(8,128)(2,1)} copy(bf16[32,512]{1,0:T(8,128)(2,1)} %get-tuple-element.10) | data formatting | bytes 65536
  110.7 1.6 %copy.19 = bf16[2,32,1024]{2,1,0:T(8,128)(2,1)} copy(bf16[2,32,1024]{2,1,0:T(8,128)(2,1)} %bitcast.14) | data formatting | bytes 262144
  (2 shorter events, 0.0 us)

commit v2 on v1

--- a/solution.py
+++ b/solution.py
@@ -27,19 +27,23 @@
     tok_ref, hid_ref, vis_ref, kvw_ref, qw_ref, ow_ref, ck_ref, cv_ref,
     span_ref, out_ref,
     qw_v, kvw_v, ow_v, ck_v, cv_v, vt_v, vts_v,
-    part, qrecv, tokg, spart, srecv, gath, obuf, orecv, mlbuf, mlrecv, att, xbuf, xrecv,
+    part, qpair, qrecv, tokg, spart, spair, srecv, gath, oacc, mlacc,
+    obuf, orecv, mlbuf, mlrecv, att, xbuf, xrecv,
     qw_sem, kvw_sem, ow_sem, c_sem, own_sem,
-    tok_s, tok_r, fwd_s, q_s, q_r, sp_s, sp_r, g_s, g_r, o_s, o_r, ml_s, ml_r, a_s, a_r, x_s, x_r,
+    tok_s, tok_r, fwd_s, qp_s, qp_r, q_s, q_r, spp_s, spp_r, sp_s, sp_r,
+    g_s, g_r, gp_s, o_s, o_r, ml_s, ml_r, a_s, a_r, ap_s, x_s, x_r,
 ):
     f32, bf16 = jnp.float32, jnp.bfloat16
     me = lax.axis_index("seq")
     w = lax.axis_index("width")
     other = 1 - w
-    r = part.shape[1]
+    parity, col, half = lax.rem(me, 2), me // 2, n // 2
+    pair = me + 1 - 2 * parity
+    r = part.shape[2]
     heads = kvw_v.shape[1] // (2 * HD)
     grouped = QH // KVH
     qcols = qw_ref.shape[1]
-    ccols = part.shape[2]
+    ccols = part.shape[3]
     tiles = qcols // tile
     feats = hid_ref.shape[1]
     lanes = grouped * r
@@ -53,6 +57,46 @@
             return carry
 
         lax.fori_loop(1, n, step, 0)
+
+    def mates(body):
+        def step(d, carry):
+            k = lax.rem(col + d, half)
+            body(k, 2 * k + parity)
+            return carry
+
+        lax.fori_loop(1, half, step, 0)
+
+    def spread(buf, send, pass_on, recv):
+        at_pair = {"seq": pair}
+        mates(lambda k, j: remote(buf.at[me], buf.at[me], send.at[k], recv.at[me], {"seq": j}).start())
+        remote(buf.at[me], buf.at[me], pass_on.at[col], recv.at[me], at_pair).start()
+
+    def relay(buf, send, pass_on, recv):
+        def one(k, j):
+            remote(buf.at[j], buf.at[j], send.at[k], recv.at[j], {"seq": j}).wait_recv()
+            remote(buf.at[j], buf.at[j], pass_on.at[k], recv.at[j], {"seq": pair}).start()
+
+        mates(one)
+
+    def collect(buf, pass_on, recv):
+        def one(k, carry):
+            j = 2 * k + 1 - parity
+            remote(buf.at[j], buf.at[j], pass_on.at[k], recv.at[j], {"seq": pair}).wait_recv()
+            return carry
+
+        lax.fori_loop(0, half, one, 0)
+
+    def spread_sent(buf, send, pass_on, recv):
+        mates(
+            lambda k, j: remote(buf.at[me], buf.at[me], send.at[k], recv.at[me], {"seq": j}).wait_send()
+        )
+
+        def one(k, carry):
+            j = 2 * k + parity
+            remote(buf.at[j], buf.at[j], pass_on.at[k], recv.at[j], {"seq": pair}).wait_send()
+            return carry
+
+        lax.fori_loop(0, half, one, 0)
 
     def qw_copy(t):
         cols = pl.ds(pl.multiple_of(t * tile, tile), tile)
@@ -95,46 +139,63 @@
         @pl.when(dest != me)
         def _():
             remote(
-                tok_ref.at[:, cols], tokg.at[me], tok_s.at[k], tok_r.at[me], {"seq": dest}
+                tok_ref.at[:, cols], tokg.at[parity, col], tok_s.at[k], tok_r.at[me], {"seq": dest}
             ).start()
 
         @pl.when(dest == me)
         def _():
-            pltpu.make_async_copy(tok_ref.at[:, cols], tokg.at[me], own_sem).start()
+            pltpu.make_async_copy(tok_ref.at[:, cols], tokg.at[parity, col], own_sem).start()
 
         return carry
 
     lax.fori_loop(0, per_half, tok_send, 0)
 
-    def q_send(value, cols):
+    def span_cols(t):
+        return pl.ds(pl.multiple_of(t * tile, tile), tile)
+
+    def pair_copy(t):
+        cols = span_cols(t)
+        return remote(
+            part.at[1 - parity, :, :, cols], qpair.at[:, :, cols], qp_s.at[t], qp_r.at[t], {"seq": pair}
+        )
+
+    def q_send(value, t):
+        cols = span_cols(t)
         for j in range(n):
-            part[j, :, cols] = value[j * r : (j + 1) * r]
-        peers(
-            lambda j: remote(
-                part.at[j, :, cols], qrecv.at[me, :, cols], q_s.at[j], q_r.at[me], {"seq": j}
+            part[j % 2, j // 2, :, cols] = value[j * r : (j + 1) * r]
+        pair_copy(t).start()
+
+    def q_tile(t, carry):
+        qw_copy(t).wait()
+        q_send(jnp.dot(hid_ref[...], qw_v[t], preferred_element_type=f32), t)
+        return carry
+
+    lax.fori_loop(0, tiles, q_tile, 0)
+    kvw_copy.wait()
+    q_send(jnp.dot(hid_ref[...], kvw_v[...], preferred_element_type=f32), tiles)
+
+    def q_on(t, carry):
+        cols = span_cols(t)
+        pair_copy(t).wait_recv()
+        part[parity, :, :, cols] = part[parity, :, :, cols] + qpair[:, :, cols]
+        mates(
+            lambda k, j: remote(
+                part.at[parity, k, :, cols], qrecv.at[col, :, cols], q_s.at[k], q_r.at[col], {"seq": j}
             ).start()
         )
-
-    def q_tile(t, carry):
-        qw_copy(t).wait()
-        value = jnp.dot(hid_ref[...], qw_v[t], preferred_element_type=f32)
-        q_send(value, pl.ds(pl.multiple_of(t * tile, tile), tile))
-        return carry
-
-    lax.fori_loop(0, tiles, q_tile, 0)
-    kvw_copy.wait()
-    q_send(
-        jnp.dot(hid_ref[...], kvw_v[...], preferred_element_type=f32), pl.ds(qcols, ccols - qcols)
-    )
+        return carry
+
+    lax.fori_loop(0, tiles + 1, q_on, 0)
 
     holder = w == me // per_half
 
     def tok_recv(i, device):
-        return remote(tokg.at[i], tokg.at[i], fwd_s.at[i], tok_r.at[i], device)
+        block = tokg.at[lax.rem(i, 2), i // 2]
+        return remote(block, block, fwd_s.at[i], tok_r.at[i], device)
 
     @pl.when(holder)
     def _():
-        pltpu.make_async_copy(tokg.at[me], tokg.at[me], own_sem).wait()
+        pltpu.make_async_copy(tokg.at[parity, col], tokg.at[parity, col], own_sem).wait()
 
         def pass_on(d, carry):
             i = lax.rem(me + d, n)
@@ -156,66 +217,98 @@
 
         lax.fori_loop(0, n, take, 0)
 
-    group = min(n, 8)
-
-    def span_chunk(c, carry):
-        rows = tokg[pl.ds(c * group, group)].reshape(group * toks, feats)
-        value = jnp.dot(rows, kvw_v[...], preferred_element_type=f32)
-        spart[pl.ds(c * group, group)] = value.reshape(group, toks, value.shape[1])
-        return carry
-
-    lax.fori_loop(0, n // group, span_chunk, 0)
-    peers(
-        lambda j: remote(spart.at[j], srecv.at[me], sp_s.at[j], sp_r.at[me], {"seq": j}).start()
-    )
-
-    qrecv[me] = part[me]
-    peers(lambda j: remote(part.at[j], qrecv.at[j], q_s.at[j], q_r.at[j], {"seq": j}).wait_recv())
-    total = lax.fori_loop(1, n, lambda i, acc: acc + qrecv[i], qrecv[0])
+    group = min(half, 8)
+
+    def span_part(side):
+        def chunk(c, carry):
+            rows = tokg[side, pl.ds(c * group, group)].reshape(group * toks, feats)
+            value = jnp.dot(rows, kvw_v[...], preferred_element_type=f32)
+            spart[side, pl.ds(c * group, group)] = value.reshape(group, toks, value.shape[1])
+            return carry
+
+        lax.fori_loop(0, half // group, chunk, 0)
+
+    span_part(1 - parity)
+    span_pair = remote(spart.at[1 - parity], spair, spp_s, spp_r, {"seq": pair})
+    span_pair.start()
+    span_part(parity)
+
+    qrecv[col] = part[parity, col]
+    mates(
+        lambda k, j: remote(
+            part.at[parity, k], qrecv.at[k], q_s.at[k], q_r.at[k], {"seq": j}
+        ).wait_recv()
+    )
+    total = lax.fori_loop(1, half, lambda i, acc: acc + qrecv[i], qrecv[0])
     gath[me] = jnp.concatenate(
         [total[:, c * HD : (c + 1) * HD] for c in range(ccols // HD)], axis=0
     ).astype(bf16)
-    peers(lambda j: remote(gath.at[me], gath.at[me], g_s.at[j], g_r.at[me], {"seq": j}).start())
+    spread(gath, g_s, gp_s, g_r)
+
+    span_pair.wait_recv()
+    spart[parity] = spart[parity] + spair[...]
+    mates(
+        lambda k, j: remote(
+            spart.at[parity, k], srecv.at[col], sp_s.at[k], sp_r.at[col], {"seq": j}
+        ).start()
+    )
+    relay(gath, g_s, gp_s, g_r)
 
     ck_copy.wait()
     cv_copy.wait()
     for h in range(heads):
         vt_v[h] = cv_v[:, h * HD : (h + 1) * HD].astype(f32).T.astype(bf16)
 
-    srecv[me] = spart[me]
-    peers(lambda j: remote(spart.at[j], srecv.at[j], sp_s.at[j], sp_r.at[j], {"seq": j}).wait_recv())
-    span = lax.fori_loop(1, n, lambda i, acc: acc + srecv[i], srecv[0]).astype(bf16)
-    span_ref[...] = span
-    for h in range(heads):
-        vts_v[h] = span[:, (2 * h + 1) * HD : (2 * h + 2) * HD].astype(f32).T.astype(bf16)
-
-    peers(lambda j: remote(gath.at[j], gath.at[j], g_s.at[j], g_r.at[j], {"seq": j}).wait_recv())
+    srecv[col] = spart[parity, col]
+    collect(gath, gp_s, g_r)
 
     slots = ck_v.shape[0]
     anchor = me * slots
     jc = max(1, min(n, 256 // lanes))
     width = jc * lanes
 
-    def attend(c, carry):
+    def queries(c, h):
+        return gath[pl.ds(c * jc, jc), h * lanes : (h + 1) * lanes, :].reshape(width, HD)
+
+    def attend_cache(c, carry):
         visible = vis_ref[pl.ds(c, 1)] - anchor
         for h in range(heads):
-            q = gath[pl.ds(c * jc, jc), h * lanes : (h + 1) * lanes, :].reshape(width, HD)
-            s1 = lax.dot_general(
-                ck_v[:, h * HD : (h + 1) * HD], q, NT, preferred_element_type=f32
+            s = lax.dot_general(
+                ck_v[:, h * HD : (h + 1) * HD], queries(c, h), NT, preferred_element_type=f32
             ) * factor
-            s2 = lax.dot_general(
-                span_ref[:, 2 * h * HD : (2 * h + 1) * HD], q, NT, preferred_element_type=f32
+            place = lax.broadcasted_iota(jnp.int32, s.shape, 0)
+            s = jnp.where(place < visible, s, MASKED)
+            m = jnp.max(s, axis=0, keepdims=True)
+            e = jnp.exp(s - m)
+            mlacc[c, h : h + 1] = m
+            mlacc[c, heads + h : heads + h + 1] = jnp.sum(e, axis=0, keepdims=True)
+            oacc[c, h] = jnp.dot(vt_v[h], e.astype(bf16), preferred_element_type=f32)
+        return carry
+
+    lax.fori_loop(0, n // jc, attend_cache, 0)
+
+    mates(
+        lambda k, j: remote(
+            spart.at[parity, k], srecv.at[k], sp_s.at[k], sp_r.at[k], {"seq": j}
+        ).wait_recv()
+    )
+    span = lax.fori_loop(1, half, lambda i, acc: acc + srecv[i], srecv[0]).astype(bf16)
+    span_ref[...] = span
+    for h in range(heads):
+        vts_v[h] = span[:, (2 * h + 1) * HD : (2 * h + 2) * HD].astype(f32).T.astype(bf16)
+
+    def attend_span(c, carry):
+        for h in range(heads):
+            s = lax.dot_general(
+                span_ref[:, 2 * h * HD : (2 * h + 1) * HD], queries(c, h), NT, preferred_element_type=f32
             ) * factor
-            place = lax.broadcasted_iota(jnp.int32, s1.shape, 0)
-            s1 = jnp.where(place < visible, s1, MASKED)
-            m = jnp.maximum(
-                jnp.max(s1, axis=0, keepdims=True), jnp.max(s2, axis=0, keepdims=True)
-            )
-            w1 = jnp.exp(s1 - m)
-            w2 = jnp.exp(s2 - m)
-            l = jnp.sum(w1, axis=0, keepdims=True) + jnp.sum(w2, axis=0, keepdims=True)
-            o = jnp.dot(vt_v[h], w1.astype(bf16), preferred_element_type=f32)
-            o = (o + jnp.dot(vts_v[h], w2.astype(bf16), preferred_element_type=f32)).astype(bf16)
+            m0 = mlacc[c, h : h + 1]
+            m = jnp.maximum(m0, jnp.max(s, axis=0, keepdims=True))
+            keep = jnp.exp(m0 - m)
+            e = jnp.exp(s - m)
+            l = mlacc[c, heads + h : heads + h + 1] * keep + jnp.sum(e, axis=0, keepdims=True)
+            o = jnp.dot(vts_v[h], e.astype(bf16), preferred_element_type=f32)
+            o = (oacc[c, h] * keep + o).astype(bf16)
             for k in range(jc):
                 cut = slice(k * lanes, (k + 1) * lanes)
                 obuf[c * jc + k, h] = o[:, cut]
@@ -231,7 +324,7 @@
 
         return carry
 
-    lax.fori_loop(0, n // jc, attend, 0)
+    lax.fori_loop(0, n // jc, attend_span, 0)
 
     per_step = n // steps
     step = me // per_step
@@ -277,10 +370,11 @@
         ready = (o / l).T
         pieces += [ready[g * r : (g + 1) * r] for g in range(grouped)]
     att[me] = jnp.concatenate(pieces, axis=1).astype(bf16)
-    peers(lambda j: remote(att.at[me], att.at[me], a_s.at[j], a_r.at[me], {"seq": j}).start())
+    spread(att, a_s, ap_s, a_r)
     for copy in ow_copies:
         copy.wait()
-    peers(lambda j: remote(att.at[j], att.at[j], a_s.at[j], a_r.at[j], {"seq": j}).wait_recv())
+    relay(att, a_s, ap_s, a_r)
+    collect(att, ap_s, a_r)
     rows = jnp.concatenate([att[j].astype(f32) for j in range(n)], axis=0).astype(bf16)
     own = out_ref.shape[1]
     cut = min(own, 256)
@@ -305,7 +399,7 @@
         @pl.when(dest != me)
         def _():
             remote(
-                tok_ref.at[:, cols], tokg.at[me], tok_s.at[k], tok_r.at[me], {"seq": dest}
+                tok_ref.at[:, cols], tokg.at[parity, col], tok_s.at[k], tok_r.at[me], {"seq": dest}
             ).wait_send()
 
         return carry
@@ -320,14 +414,26 @@
 
         lax.fori_loop(0, n, passed, 0)
 
+    def pair_sent(t, carry):
+        pair_copy(t).wait_send()
+        return carry
+
+    lax.fori_loop(0, tiles + 1, pair_sent, 0)
+    span_pair.wait_send()
+
+    def sums_sent(k, j):
+        at = {"seq": j}
+        remote(part.at[parity, k], qrecv.at[col], q_s.at[k], q_r.at[col], at).wait_send()
+        remote(spart.at[parity, k], srecv.at[col], sp_s.at[k], sp_r.at[col], at).wait_send()
+
+    mates(sums_sent)
+    spread_sent(gath, g_s, gp_s, g_r)
+    spread_sent(att, a_s, ap_s, a_r)
+
     def sent(j):
         at = {"seq": j}
-        remote(part.at[j], qrecv.at[me], q_s.at[j], q_r.at[me], at).wait_send()
-        remote(spart.at[j], srecv.at[me], sp_s.at[j], sp_r.at[me], at).wait_send()
-        remote(gath.at[me], gath.at[me], g_s.at[j], g_r.at[me], at).wait_send()
         remote(mlbuf.at[j], mlrecv.at[me], ml_s.at[j], ml_r.at[me], at).wait_send()
         remote(obuf.at[j], orecv.at[me], o_s.at[j], o_r.at[me], at).wait_send()
-        remote(att.at[me], att.at[me], a_s.at[j], a_r.at[me], at).wait_send()
 
     peers(sent)
     swap.wait_send()
@@ -348,7 +454,8 @@
     heads = kvc // (2 * HD)
     qcols = query_weight.shape[1]
     ccols = qcols + kvc
-    tile = min(qcols, 512)
+    tile = kvc
+    half = n // 2
     slots = cache_keys.shape[0]
     own = out_weight.shape[1] // mesh.shape["width"]
     f32, bf16 = jnp.float32, jnp.bfloat16
@@ -377,12 +484,16 @@
             pltpu.VMEM((slots, heads * HD), bf16),
             pltpu.VMEM((heads, HD, slots), bf16),
             pltpu.VMEM((heads, HD, toks), bf16),
-            pltpu.VMEM((n, r, ccols), f32),
-            pltpu.VMEM((n, r, ccols), f32),
-            pltpu.VMEM((n, toks, feats), bf16),
-            pltpu.VMEM((n, toks, kvc), f32),
-            pltpu.VMEM((n, toks, kvc), f32),
+            pltpu.VMEM((2, half, r, ccols), f32),
+            pltpu.VMEM((half, r, ccols), f32),
+            pltpu.VMEM((half, r, ccols), f32),
+            pltpu.VMEM((2, half, toks, feats), bf16),
+            pltpu.VMEM((2, half, toks, kvc), f32),
+            pltpu.VMEM((half, toks, kvc), f32),
+            pltpu.VMEM((half, toks, kvc), f32),
             pltpu.VMEM((n, ccols // HD * r, HD), bf16),
+            pltpu.VMEM((n // jc, heads, HD, jc * lanes), f32),
+            pltpu.VMEM((n // jc, 2 * heads, jc * lanes), f32),
             pltpu.VMEM((n, heads, HD, lanes), bf16),
             pltpu.VMEM((n, heads, HD, lanes), bf16),
             pltpu.VMEM((n, 2 * heads, lanes), f32),
@@ -391,8 +502,12 @@
             pltpu.VMEM((rows, own), bf16),
             pltpu.VMEM((rows, own), bf16),
             dma((qcols // tile,)), dma, dma((ow_parts,)), dma((2,)), dma,
-            dma((n,)), dma((n,)), dma((n,)), dma((n,)), dma((n,)), dma((n,)), dma((n,)),
-            dma((n,)), dma((n,)), dma((n,)), dma((n,)), dma((n,)), dma((n,)), dma((n,)), dma((n,)),
+            dma((n,)), dma((n,)), dma((n,)),
+            dma((qcols // tile + 1,)), dma((qcols // tile + 1,)), dma((half,)), dma((half,)),
+            dma, dma, dma((half,)), dma((half,)),
+            dma((half,)), dma((n,)), dma((half,)),
+            dma((n,)), dma((n,)), dma((n,)), dma((n,)),
+            dma((half,)), dma((n,)), dma((half,)),
             dma, dma,
         ],
         compiler_params=pltpu.CompilerParams(

time: 113 us -> 92.1 us (0.82)
  Pallas kernels: 104 us -> 83.8 us
    pallas_call x1, Pallas kernels: 104 us -> 83.8 us  [local(): pl.pallas_call(functools.partial(layer, n, steps, tile), out_shape=(jax.S...]
where the time goes in v2:
time: 92.1 us; the launch traced here: 91.8 us
  Pallas kernels  83.8 us (91%)
  local copies, waits for them, and re-layouts  6.07 us (7%)
  between operations  1.29 us (1%)
    pallas_call x1, Pallas kernels, local(): pl.pallas_call(functools.partial(layer, n, steps, tile), out_shape=(jax.S...  83.8 us
    unnamed x2, local copies, waits for them, and re-layouts  2.94 us
    reshape x1, local copies, waits for them, and re-layouts, local(): cache_values.reshape(slots, heads * HD)  2.33 us

profile of v2, /device:TPU:0, one launch (start us, length us, event | category | flops | bytes accessed | tf_op | source)
XLA Modules:
  0.0 91.8 jit_solution(16729105661072872983)
XLA Ops:
  1.3 0.7 broadcast_minimum_fusion
  1.9 0.1 tile.10
  2.0 0.7 reshape.28.vis_ref
  2.7 2.3 %copy_bitcast_fusion = (bf16[1024,256]{1,0:T(8,128)(2,1)}, bf16[1024,256]{1,0:T(8,128)(2,1)}) fusion(bf16[128,8,2,128]{3,2,1,0:T(2,128)(2,1)} %bitcast.11, bf16[128,8,2,128]{3,2,1,0:T(2,128)(2,1)} %bitcast.12), kind=kLoop, calls=%fused_computation | loop fusion | bytes 2097152 | tf_op jit(solution)/shard_map/reshape | solution.py:524
  5.1 83.8 %shard_map.104 = (bf16[32,512]{1,0:T(8,128)(2,1)}, bf16[64,1024]{1,0:T(8,128)(2,1)}) custom-call(bf16[32,8192]{1,0:T(8,128)(2,1)} %tok_ref.1, bf16[64,2048]{1,0:T(8,128)(2,1)} %bitcast.13, s32[4,256]{1,0:T(4,128)} %reshape.28.vis_ref, bf16[2048,512]{1,0:T(8,128)(2,1)} %kvw_ref.1, bf16[2048,4096]{1,0:T(8,128)(2,1)} %qw_ref.1, bf16[4096,2048]{1,0:T(8,128)(2,1)} %ow_ref.1, ...), custom_call_target="tpu_custom_call" | custom-call | tf_op jit(solution)/shard_map/pallas_call | solution.py:471
  88.8 1.4 %copy.18 = bf16[32,512]{1,0:T(8,128)(2,1)} copy(bf16[32,512]{1,0:T(8,128)(2,1)} %get-tuple-element.10) | data formatting | bytes 65536
  90.2 1.6 %copy.19 = bf16[2,32,1024]{2,1,0:T(8,128)(2,1)} copy(bf16[2,32,1024]{2,1,0:T(8,128)(2,1)} %bitcast.14) | data formatting | bytes 262144
  (2 shorter events, 0.0 us)

commit v3 on v2

--- a/solution.py
+++ b/solution.py
@@ -26,8 +26,8 @@
     n, steps, tile,
     tok_ref, hid_ref, vis_ref, kvw_ref, qw_ref, ow_ref, ck_ref, cv_ref,
     span_ref, out_ref,
-    qw_v, kvw_v, ow_v, ck_v, cv_v, vt_v, vts_v,
-    part, qpair, qrecv, tokg, spart, spair, srecv, gath, oacc, mlacc,
+    qw_v, kvw_v, ow_v, ck_v, cv_v, kh_v, vt_v, vts_v,
+    part, qpair, qrecv, tokg, spart, spair, srecv, gath,
     obuf, orecv, mlbuf, mlrecv, att, xbuf, xrecv,
     qw_sem, kvw_sem, ow_sem, c_sem, own_sem,
     tok_s, tok_r, fwd_s, qp_s, qp_r, q_s, q_r, spp_s, spp_r, sp_s, sp_r,
@@ -165,15 +165,6 @@
             part[j % 2, j // 2, :, cols] = value[j * r : (j + 1) * r]
         pair_copy(t).start()
 
-    def q_tile(t, carry):
-        qw_copy(t).wait()
-        q_send(jnp.dot(hid_ref[...], qw_v[t], preferred_element_type=f32), t)
-        return carry
-
-    lax.fori_loop(0, tiles, q_tile, 0)
-    kvw_copy.wait()
-    q_send(jnp.dot(hid_ref[...], kvw_v[...], preferred_element_type=f32), tiles)
-
     def q_on(t, carry):
         cols = span_cols(t)
         pair_copy(t).wait_recv()
@@ -185,7 +176,23 @@
         )
         return carry
 
-    lax.fori_loop(0, tiles + 1, q_on, 0)
+    lag = 3
+
+    def q_tile(t, carry):
+        qw_copy(t).wait()
+        q_send(jnp.dot(hid_ref[...], qw_v[t], preferred_element_type=f32), t)
+
+        @pl.when(t >= lag)
+        def _():
+            q_on(t - lag, 0)
+
+        return carry
+
+    lax.fori_loop(0, tiles, q_tile, 0)
+    kvw_copy.wait()
+    q_send(jnp.dot(hid_ref[...], kvw_v[...], preferred_element_type=f32), tiles)
+
+    lax.fori_loop(max(tiles - lag, 0), tiles + 1, q_on, 0)
 
     holder = w == me // per_half
 
@@ -232,6 +239,12 @@
     span_pair = remote(spart.at[1 - parity], spair, spp_s, spp_r, {"seq": pair})
     span_pair.start()
     span_part(parity)
+
+    ck_copy.wait()
+    cv_copy.wait()
+    for h in range(heads):
+        vt_v[h] = cv_v[...].astype(f32)[:, h, :].T.astype(bf16)
+        kh_v[h] = ck_v[...].astype(f32)[:, h, :].astype(bf16)
 
     qrecv[col] = part[parity, col]
     mates(
@@ -254,11 +267,6 @@
     )
     relay(gath, g_s, gp_s, g_r)
 
-    ck_copy.wait()
-    cv_copy.wait()
-    for h in range(heads):
-        vt_v[h] = cv_v[:, h * HD : (h + 1) * HD].astype(f32).T.astype(bf16)
-
     srecv[col] = spart[parity, col]
     collect(gath, gp_s, g_r)
 
@@ -270,23 +278,6 @@
     def queries(c, h):
         return gath[pl.ds(c * jc, jc), h * lanes : (h + 1) * lanes, :].reshape(width, HD)
 
-    def attend_cache(c, carry):
-        visible = vis_ref[pl.ds(c, 1)] - anchor
-        for h in range(heads):
-            s = lax.dot_general(
-                ck_v[:, h * HD : (h + 1) * HD], queries(c, h), NT, preferred_element_type=f32
-            ) * factor
-            place = lax.broadcasted_iota(jnp.int32, s.shape, 0)
-            s = jnp.where(place < visible, s, MASKED)
-            m = jnp.max(s, axis=0, keepdims=True)
-            e = jnp.exp(s - m)
-            mlacc[c, h : h + 1] = m
-            mlacc[c, heads + h : heads + h + 1] = jnp.sum(e, axis=0, keepdims=True)
-            oacc[c, h] = jnp.dot(vt_v[h], e.astype(bf16), preferred_element_type=f32)
-        return carry
-
-    lax.fori_loop(0, n // jc, attend_cache, 0)
-
     mates(
         lambda k, j: remote(
             spart.at[parity, k], srecv.at[k], sp_s.at[k], sp_r.at[k], {"seq": j}
@@ -297,18 +288,25 @@
     for h in range(heads):
         vts_v[h] = span[:, (2 * h + 1) * HD : (2 * h + 2) * HD].astype(f32).T.astype(bf16)
 
-    def attend_span(c, carry):
+    def attend(i, carry):
+        c = lax.rem(me // jc + 1 + i, n // jc)
+        visible = vis_ref[pl.ds(c, 1)] - anchor
         for h in range(heads):
-            s = lax.dot_general(
-                span_ref[:, 2 * h * HD : (2 * h + 1) * HD], queries(c, h), NT, preferred_element_type=f32
+            q = queries(c, h)
+            s1 = lax.dot_general(kh_v[h], q, NT, preferred_element_type=f32) * factor
+            s2 = lax.dot_general(
+                span_ref[:, 2 * h * HD : (2 * h + 1) * HD], q, NT, preferred_element_type=f32
             ) * factor
-            m0 = mlacc[c, h : h + 1]
-            m = jnp.maximum(m0, jnp.max(s, axis=0, keepdims=True))
-            keep = jnp.exp(m0 - m)
-            e = jnp.exp(s - m)
-            l = mlacc[c, heads + h : heads + h + 1] * keep + jnp.sum(e, axis=0, keepdims=True)
-            o = jnp.dot(vts_v[h], e.astype(bf16), preferred_element_type=f32)
-            o = (oacc[c, h] * keep + o).astype(bf16)
+            place = lax.broadcasted_iota(jnp.int32, s1.shape, 0)
+            s1 = jnp.where(place < visible, s1, MASKED)
+            m = jnp.maximum(
+                jnp.max(s1, axis=0, keepdims=True), jnp.max(s2, axis=0, keepdims=True)
+            )
+            w1 = jnp.exp(s1 - m)
+            w2 = jnp.exp(s2 - m)
+            l = jnp.sum(w1, axis=0, keepdims=True) + jnp.sum(w2, axis=0, keepdims=True)
+            o = jnp.dot(vt_v[h], w1.astype(bf16), preferred_element_type=f32)
+            o = (o + jnp.dot(vts_v[h], w2.astype(bf16), preferred_element_type=f32)).astype(bf16)
             for k in range(jc):
                 cut = slice(k * lanes, (k + 1) * lanes)
                 obuf[c * jc + k, h] = o[:, cut]
@@ -324,7 +322,7 @@
 
         return carry
 
-    lax.fori_loop(0, n // jc, attend_span, 0)
+    lax.fori_loop(0, n // jc, attend, 0)
 
     per_step = n // steps
     step = me // per_step
@@ -359,14 +357,14 @@
     pieces = []
     for h in range(heads):
         m0, l0, o0 = fresh[h]
-        top = lax.fori_loop(0, n, lambda i, a: jnp.maximum(a, mlrecv[i, h : h + 1]), m0)
+        tops, sums = mlrecv[:, h, :], mlrecv[:, heads + h, :]
+        top = jnp.maximum(m0, jnp.max(tops, axis=0, keepdims=True))
         keep = jnp.exp(m0 - top)
-
-        def fold(i, acc):
-            k = jnp.exp(mlrecv[i, h : h + 1] - top)
-            return acc[0] + mlrecv[i, heads + h : heads + h + 1] * k, acc[1] + orecv[i, h].astype(f32) * k
-
-        l, o = lax.fori_loop(0, n, fold, (l0 * keep, o0 * keep))
+        weight = jnp.exp(tops - top)
+        l = l0 * keep + jnp.sum(sums * weight, axis=0, keepdims=True)
+        o = o0 * keep
+        for i in range(n):
+            o = o + orecv[i, h].astype(f32) * weight[i : i + 1]
         ready = (o / l).T
         pieces += [ready[g * r : (g + 1) * r] for g in range(grouped)]
     att[me] = jnp.concatenate(pieces, axis=1).astype(bf16)
@@ -480,8 +478,9 @@
             pltpu.VMEM((qcols // tile, feats, tile), bf16),
             pltpu.VMEM((feats, kvc), bf16),
             pltpu.VMEM(out_weight.shape, bf16),
-            pltpu.VMEM((slots, heads * HD), bf16),
-            pltpu.VMEM((slots, heads * HD), bf16),
+            pltpu.VMEM((slots, heads, HD), bf16),
+            pltpu.VMEM((slots, heads, HD), bf16),
+            pltpu.VMEM((heads, slots, HD), bf16),
             pltpu.VMEM((heads, HD, slots), bf16),
             pltpu.VMEM((heads, HD, toks), bf16),
             pltpu.VMEM((2, half, r, ccols), f32),
@@ -492,8 +491,6 @@
             pltpu.VMEM((half, toks, kvc), f32),
             pltpu.VMEM((half, toks, kvc), f32),
             pltpu.VMEM((n, ccols // HD * r, HD), bf16),
-            pltpu.VMEM((n // jc, heads, HD, jc * lanes), f32),
-            pltpu.VMEM((n // jc, 2 * heads, jc * lanes), f32),
             pltpu.VMEM((n, heads, HD, lanes), bf16),
             pltpu.VMEM((n, heads, HD, lanes), bf16),
             pltpu.VMEM((n, 2 * heads, lanes), f32),
@@ -520,8 +517,8 @@
         kv_weight,
         query_weight,
         out_weight,
-        cache_keys.reshape(slots, heads * HD),
-        cache_values.reshape(slots, heads * HD),
+        cache_keys,
+        cache_values,
     )
     return span_kv, out.reshape(steps, branches, own)
 

time: 92.1 us -> 86.7 us (0.941)
  Pallas kernels: 83.8 us -> 80.4 us
  local copies, waits for them, and re-layouts: 6.07 us -> 3.73 us
    pallas_call x1, Pallas kernels: 83.8 us -> 80.4 us  [local(): pl.pallas_call(functools.partial(layer, n, steps, tile), out_shape=(jax.S...]
    reshape x1 -> x0, local copies, waits for them, and re-layouts: 2.33 us -> none  [local(): cache_values.reshape(slots, heads * HD)]
where the time goes in v3:
time: 86.7 us; the launch traced here: 86.1 us
  Pallas kernels  80.4 us (93%)
  local copies, waits for them, and re-layouts  3.73 us (4%)
  between operations  1.29 us (1%)
    pallas_call x1, Pallas kernels, local(): pl.pallas_call(functools.partial(layer, n, steps, tile), out_shape=(jax.S...  80.4 us
    unnamed x2, local copies, waits for them, and re-layouts  2.94 us

profile of v3, /device:TPU:0, one launch (start us, length us, event | category | flops | bytes accessed | tf_op | source)
XLA Modules:
  0.0 86.1 jit_solution(18119234185554594897)
XLA Ops:
  1.3 0.7 broadcast_minimum_fusion
  1.9 0.1 tile.10
  2.0 0.7 reshape.22.vis_ref
  2.7 80.4 %shard_map.104 = (bf16[32,512]{1,0:T(8,128)(2,1)}, bf16[64,1024]{1,0:T(8,128)(2,1)}) custom-call(bf16[32,8192]{1,0:T(8,128)(2,1)} %tok_ref.1, bf16[64,2048]{1,0:T(8,128)(2,1)} %bitcast.5, s32[4,256]{1,0:T(4,128)} %reshape.22.vis_ref, bf16[2048,512]{1,0:T(8,128)(2,1)} %kvw_ref.1, bf16[2048,4096]{1,0:T(8,128)(2,1)} %qw_ref.1, bf16[4096,2048]{1,0:T(8,128)(2,1)} %ow_ref.1, ...), custom_call_target="tpu_custom_call" | custom-call | tf_op jit(solution)/shard_map/pallas_call | solution.py:469
  83.2 1.4 %copy.14 = bf16[32,512]{1,0:T(8,128)(2,1)} copy(bf16[32,512]{1,0:T(8,128)(2,1)} %get-tuple-element.8) | data formatting | bytes 65536
  84.5 1.6 %copy.15 = bf16[2,32,1024]{2,1,0:T(8,128)(2,1)} copy(bf16[2,32,1024]{2,1,0:T(8,128)(2,1)} %bitcast.6) | data formatting | bytes 262144
  (2 shorter events, 0.0 us)
